TPU v7x, 32 devices: a whole 2x2x4 slice. The times are simulated.
32 devices in a mesh: groups: 2 (over y), shard: 4 (over z), section: 2 (over x), halo: 2 (over core).
Axes of the slice: x: 2, y: 2, z: 4, core: 2. Of those that a mesh axis runs over, the one named last changes fastest.
Arguments:
- features: bfloat16 [4, 4, 16, 64, 320], P(('groups', 'section'), 'shard', 'halo'), parts along dimension 0, may hold values from -6 to 6
- timesteps: int32 [4, 2], P(('groups', 'section')), parts along dimension 0, may hold values from 0 to 999
- conv_first: bfloat16 [2, 3, 3, 320, 320], P('section'), may hold values from -0.109375 to 0.109375
- conv_second: bfloat16 [2, 3, 3, 320, 320], P('section'), may hold values from -0.109375 to 0.109375
- time_weight: bfloat16 [2, 320, 320], P('section'), may hold values from -0.3125 to 0.3125
- qkv_weight: bfloat16 [2, 320, 960], P('section'), may hold values from -7 to 7
- attn_out: bfloat16 [2, 320, 320], P('section'), may hold values from -0.3125 to 0.3125
- geglu_in: bfloat16 [2, 320, 2560], P('section'), may hold values from -0.3125 to 0.3125
- geglu_out: bfloat16 [2, 1280, 320], P('section'), may hold values from -0.15625 to 0.15625
Outputs:
- result: bfloat16 [4, 4, 16, 64, 320], P(('groups', 'section'), 'shard', 'halo'), parts along dimension 0
There are 2 independent parts, one for each index of `groups`. A program takes and returns all parts, laid end to end along the dimension named above; an argument that names none is the same for every part. Nothing has to cross between parts.
All inputs are finite; a program needn't handle non-finite values.
Results may differ from a plain program's by a relative error of at most 0.02.
Values may be sent and summed in bfloat16 or wider, within the bound.
A program may use at most 64 MiB of HBM per device.

v0:
```python
import functools
import math

import jax
import jax.numpy as jnp
from jax import lax
from jax.experimental import pallas as pl
from jax.experimental.pallas import tpu as pltpu
from jax.sharding import PartitionSpec as P

HEAD_DIM = 64
GROUPS = 32
STEPS = 2
MESH = pl.DeviceIdType.MESH
F32 = jnp.float32
BF16 = jnp.bfloat16
BLK = 64
SUBS = 2
UNROLL = 4
SHIFTS = 4
PAD = 8


def matmul(a, b):
    return jnp.dot(a, b, preferred_element_type=F32)


def matmul_t(a, b):
    return lax.dot_general(a, b, (((1,), (1,)), ((), ())), preferred_element_type=F32)


def silu(u):
    return u * (1.0 / (1.0 + jnp.exp(-u)))


def kernel(dims, stamps, feat, cf_h, cs_h, tw_h, qkv_h, ao_h, gi_h, go_h, out, *scratch):
    (rows, width, chans, inner, nsh, nsec, subs) = dims
    (F, FX, first_rx, H, G, A, S, PB, O, stat_tx, stat_rx, edge_x, edge_h, emb, gmask, hmask, hmask_t,
     N, Q, K, V, PH, PL, OB, S2, ACT,
     cf, cs, tw, qkv, ao, gi, go,
     w_sem, x_send, x_recv, first_send, first_recv, halo_send, halo_recv, in_send, in_recv, out_send, out_recv, own_sem) = scratch
    tokens = rows * width
    part = tokens // nsh
    sub = part // subs
    crowd = nsh * sub
    rim = (rows + 2) * width
    me = lax.axis_index("shard")
    sec = lax.axis_index("section")
    side = lax.axis_index("halo")
    nxt = lax.rem(sec + 1, nsec)

    own = pltpu.make_async_copy(feat, FX, w_sem.at[7])
    own.start()
    loads = [
        pltpu.make_async_copy(src, dst, w_sem.at[i])
        for i, (src, dst) in enumerate(
            ((cf_h, cf), (cs_h, cs), (tw_h, tw), (qkv_h, qkv), (ao_h, ao), (gi_h, gi), (go_h, go))
        )
    ]
    for load in loads:
        load.start()

    def at(shard, section):
        return {"shard": shard, "section": section}

    barrier = pltpu.get_barrier_semaphore()
    peers = [{"halo": 1 - side}]
    for d in range(1, nsh):
        peers.append(at(lax.rem(me + d, nsh), sec))
    for e in sorted({1 % nsec, (nsec - 1) % nsec} - {0}):
        for d in range(nsh):
            peers.append(at(lax.rem(me + d, nsh), lax.rem(sec + e, nsec)))
        peers.append({"section": lax.rem(sec + e, nsec), "halo": 1 - side})
    for peer in peers:
        pl.semaphore_signal(barrier, inc=1, device_id=peer, device_id_type=MESH)
    pl.semaphore_wait(barrier, len(peers))

    edge_at = pl.multiple_of((1 - side) * (tokens - width), 16)
    piece = tokens // SHIFTS
    shifts = [
        pltpu.make_async_remote_copy(
            src_ref=feat.at[pl.ds(i * piece, piece)], dst_ref=F.at[0, pl.ds(i * piece, piece)],
            send_sem=x_send.at[i], recv_sem=x_recv.at[i],
            device_id={"section": nxt}, device_id_type=MESH,
        )
        for i in range(SHIFTS)
    ]
    firsts = [
        pltpu.make_async_remote_copy(
            src_ref=src, dst_ref=dst, send_sem=first_send.at[i], recv_sem=first_recv.at[i],
            device_id={"section": nxt, "halo": core}, device_id_type=MESH,
        )
        for i, (src, dst, core) in enumerate((
            (stat_tx.at[0], first_rx.at[0], side),
            (stat_tx.at[0], first_rx.at[1], 1 - side),
            (feat.at[pl.ds(edge_at, width)], edge_x.at[0], 1 - side),
        ))
    ]
    firsts[2].start()
    for i in range(SHIFTS // 2):
        shifts[i].start()
    stat_tx[...] = jnp.zeros_like(stat_tx)

    def fold(carry, v):
        s1, s2 = carry
        v = v.reshape(v.shape[0] // 8, 8, chans)
        return s1 + jnp.sum(v, axis=0), s2 + jnp.sum(v * v, axis=0)

    none = (jnp.zeros((8, chans), F32), jnp.zeros((8, chans), F32))

    def publish(slot, sums):
        stat_tx[slot, 0:1, :] = jnp.sum(sums[0], axis=0, keepdims=True)
        stat_tx[slot, 1:2, :] = jnp.sum(sums[1], axis=0, keepdims=True)

    own.wait()

    def own_total(i, carry):
        return fold(carry, FX[pl.ds(pl.multiple_of(i * BLK, BLK), BLK), :].astype(F32))
    publish(0, lax.fori_loop(0, tokens // BLK, own_total, none, unroll=UNROLL))
    firsts[0].start()
    firsts[1].start()
    for i in range(SHIFTS // 2, SHIFTS):
        shifts[i].start()

    per = chans // GROUPS
    ci = lax.broadcasted_iota(jnp.int32, (chans, chans), 0)
    cj = lax.broadcasted_iota(jnp.int32, (chans, chans), 1)
    gmask[...] = jnp.where(ci - lax.rem(ci, per) == cj - lax.rem(cj, per), 1.0, 0.0).astype(F32)
    lanes = hmask.shape[1]
    hi_ = lax.broadcasted_iota(jnp.int32, (chans, lanes), 0)
    hj_ = lax.broadcasted_iota(jnp.int32, (chans, lanes), 1)
    hmask[...] = jnp.where(hi_ - lax.rem(hi_, HEAD_DIM) == hj_ * HEAD_DIM, HEAD_DIM ** (-0.5), 0.0).astype(BF16)
    ti_ = lax.broadcasted_iota(jnp.int32, (lanes, chans), 0)
    tj_ = lax.broadcasted_iota(jnp.int32, (lanes, chans), 1)
    hmask_t[...] = jnp.where(tj_ - lax.rem(tj_, HEAD_DIM) == ti_ * HEAD_DIM, 1.0, 0.0).astype(BF16)
    zeros_rim = jnp.zeros((width, chans), F32)
    G[pl.ds(0, PAD), :] = jnp.zeros((PAD, chans), F32)
    G[pl.ds(PAD + rim, PAD), :] = jnp.zeros((PAD, chans), F32)
    G[pl.ds(PAD, width), :] = zeros_rim
    G[pl.ds(PAD + rim - width, width), :] = zeros_rim

    loads[2].wait()
    half = chans // 2
    lane = lax.broadcasted_iota(jnp.int32, (16, chans), 1)
    k_of = jnp.where(lane < half, lane, lane - half).astype(F32)
    frequency = jnp.exp(-math.log(10000.0) * k_of / half)
    for n in range(STEPS):
        angles = stamps[0, n].astype(F32) * frequency
        wave = jnp.where(lane < half, jnp.cos(angles), jnp.sin(angles))
        emb[n] = matmul(silu(wave).astype(BF16), tw[...])

    rim_at = pl.multiple_of(PAD + (1 - side) * (rim - width), 8)
    count = float(rows * 2 * width * per)

    def swap(slot, edge_src, edge_dst):
        copies = [
            pltpu.make_async_remote_copy(
                src_ref=src, dst_ref=dst, send_sem=halo_send.at[slot, i], recv_sem=halo_recv.at[slot, i],
                device_id={"halo": 1 - side}, device_id_type=MESH,
            )
            for i, (src, dst) in enumerate(
                ((edge_src, edge_dst), (stat_tx.at[slot], stat_rx.at[slot]))
            )
        ]
        return copies

    def moments(both):
        summed = jnp.dot(both, gmask[...], preferred_element_type=F32, precision=lax.Precision.HIGHEST)
        average = summed[0:1, :] / count
        second = summed[1:2, :] / count
        return average, lax.rsqrt(second - average * average + 1e-05)

    def activate(load, load_edge, both, arrivals=()):
        average, inverse = moments(both)

        def one(i, c):
            at_ = pl.multiple_of(i * BLK, BLK)
            G[pl.ds(PAD + width + at_, BLK), :] = silu((load(pl.ds(at_, BLK)) - average) * inverse)
            return c
        stages = max(len(arrivals), 1)
        for i in range(stages):
            if arrivals:
                arrivals[i].wait_recv()
            lax.fori_loop(i * (tokens // BLK) // stages, (i + 1) * (tokens // BLK) // stages, one, 0, unroll=2)
        G[pl.ds(rim_at, width), :] = silu((load_edge() - average) * inverse)
        col = lax.rem(lax.broadcasted_iota(jnp.int32, (width, chans), 0), width)

        def two(i, c):
            at_ = pl.multiple_of(i * width, width)
            window = G[pl.ds(at_, width + 2 * PAD), :]
            left = window[PAD - 1 : PAD - 1 + width]
            mid = window[PAD : PAD + width]
            right = window[PAD + 1 : PAD + 1 + width]
            dst = pl.ds(at_, width)
            A[dst, 0:chans] = jnp.where(col == 0, 0.0, left).astype(BF16)
            A[dst, chans : 2 * chans] = mid.astype(BF16)
            A[dst, 2 * chans :] = jnp.where(col == width - 1, 0.0, right).astype(BF16)
            return c
        lax.fori_loop(0, rows + 2, two, 0, unroll=5)

    def conv(weights, start, size):
        return sum(matmul(A[pl.ds(start + r * width, size), :], weights[r]) for r in range(3))

    def normalise(src):
        def one(i, c):
            at_ = pl.ds(pl.multiple_of(i * BLK, BLK), BLK)
            v = src(at_)
            centred = v - jnp.mean(v, axis=-1, keepdims=True)
            spread = jnp.mean(centred * centred, axis=-1, keepdims=True)
            N[at_, :] = (centred * lax.rsqrt(spread + 1e-05)).astype(BF16)
            return c
        lax.fori_loop(0, crowd // BLK, one, 0, unroll=UNROLL)

    def gather_copy(n, k, d):
        to = lax.rem(me + d, nsh)
        return pltpu.make_async_remote_copy(
            src_ref=S.at[n, k, to], dst_ref=PB.at[n, k, me],
            send_sem=in_send.at[n, k, d], recv_sem=in_recv.at[n, k, d],
            device_id={"shard": to}, device_id_type=MESH,
        )

    def return_copy(n, k, d):
        last = n == STEPS - 1
        target = out if last else F.at[n + 1]
        landing = target.at[pl.ds(pl.multiple_of(me * part + k * sub, 16), sub)]
        to = lax.rem(me + d, nsh)
        if d == 0 and (last or nsec == 1):
            return pltpu.make_async_copy(O.at[n, k, me], landing, own_sem.at[n, k])
        return pltpu.make_async_remote_copy(
            src_ref=O.at[n, k, to], dst_ref=landing,
            send_sem=out_send.at[n, k, d], recv_sem=out_recv.at[n, k, d],
            device_id=at(to, sec if last else nxt), device_id_type=MESH,
        )

    def pixels(n, k):
        stream = PB.at[n, k]

        def load_p(s):
            return stream.reshape(crowd, chans)[s, :].astype(F32)
        normalise(load_p)
        proj = matmul(N[...], qkv[...]).astype(BF16)
        Q[...] = proj[:, :chans].astype(F32)
        K[...] = proj[:, chans : 2 * chans].astype(F32)
        V[...] = proj[:, 2 * chans :].astype(F32)

        def frame(f, c):
            q = Q[pl.ds(pl.multiple_of(f * sub, 16), sub), :]
            start = pl.multiple_of(f * crowd, 16)
            for g in range(nsh):
                prod = q * K[g * sub : (g + 1) * sub, :]
                high = prod.astype(BF16)
                PH[pl.ds(start + g * sub, sub), :] = high
                PL[pl.ds(start + g * sub, sub), :] = (prod - high.astype(F32)).astype(BF16)
            score = matmul(PH[pl.ds(start, crowd), :], hmask[...]) + matmul(PL[pl.ds(start, crowd), :], hmask[...])
            pieces = [score[g * sub : (g + 1) * sub] for g in range(nsh)]
            top = functools.reduce(jnp.maximum, pieces)
            pieces = [jnp.exp(p - top) for p in pieces]
            scale = 1.0 / functools.reduce(jnp.add, pieces)
            weights = jnp.concatenate([(p * scale).astype(BF16) for p in pieces], axis=0)
            weights = matmul(weights, hmask_t[...])
            mixed = weights[0:sub] * V[0:sub, :]
            for g in range(1, nsh):
                mixed = mixed + weights[g * sub : (g + 1) * sub] * V[g * sub : (g + 1) * sub, :]
            OB[pl.ds(pl.multiple_of(f * sub, 16), sub), :] = mixed.astype(BF16)
            return c
        lax.fori_loop(0, nsh, frame, 0, unroll=4)

        S2[...] = (matmul(OB[...], ao[...]) + stream[...].reshape(crowd, chans).astype(F32)).astype(BF16)
        normalise(lambda s: S2[s, :].astype(F32))
        wide = 256
        for j in range(inner // wide):
            value = matmul(N[...], gi[:, j * wide : (j + 1) * wide])
            gate = matmul(N[...], gi[:, inner + j * wide : inner + (j + 1) * wide])
            gelu = 0.5 * gate * (1.0 + lax.erf(gate * (0.5 ** 0.5)))
            ACT[:, j * wide : (j + 1) * wide] = (value * gelu).astype(BF16)
        O[n, k] = (matmul_t(ACT[...], go[...]) + S2[...].astype(F32)).astype(BF16).reshape(nsh, sub, chans)

    for n in range(STEPS):
        field = F.at[n]

        def load_x(s, field=field):
            return field[s, :].astype(F32)

        if n == 0:
            for c in firsts:
                c.wait()
            activate(load_x, lambda: edge_x[0].astype(F32), first_rx[0] + first_rx[1], shifts)
            for c in shifts:
                c.wait_send()
            loads[0].wait()
        else:
            swaps = swap(2 * n, field.at[pl.ds(edge_at, width)], edge_x.at[n])
            swaps[0].start()
            publish(2 * n, sums)
            swaps[1].start()
            for c in swaps:
                c.wait()
            activate(load_x, lambda n=n: edge_x[n].astype(F32), stat_tx[2 * n] + stat_rx[2 * n])
        sums = none
        for i in range(2):
            rows_ = pl.ds(i * (tokens // 2), tokens // 2)
            h1 = conv(cf, i * (tokens // 2), tokens // 2) + emb[n, 0:1, :]
            H[n, rows_, :] = h1
            sums = fold(sums, h1)

        slot = 2 * n + 1
        swaps = swap(slot, H.at[n, pl.ds(edge_at, width)], edge_h.at[n])
        swaps[0].start()
        publish(slot, sums)
        swaps[1].start()
        for c in swaps:
            c.wait()
        activate(lambda s, n=n: H[n, s, :], lambda n=n: edge_h[n], stat_tx[slot] + stat_rx[slot])
        if n == 0:
            loads[1].wait()
        for k in range(subs):
            spans = [j * part + k * sub for j in range(nsh)]
            total = sum(
                matmul(jnp.concatenate([A[pl.ds(r * width + a, sub), :] for a in spans], axis=0), cs[r])
                for r in range(3)
            )
            base = jnp.concatenate([field[pl.ds(a, sub), :] for a in spans], axis=0)
            S[n, k] = (total + base.astype(F32)).astype(BF16).reshape(nsh, sub, chans)
            for d in range(1, nsh):
                gather_copy(n, k, d).start()
            PB[n, k, me] = S[n, k, me]

        if n == 0:
            for i in (3, 4, 5, 6):
                loads[i].wait()

        def temporal(k, carry, n=n):
            for d in range(1, nsh):
                gather_copy(n, k, d).wait_recv()
            pixels(n, k)
            for d in range(nsh):
                return_copy(n, k, d).start()
            return carry
        lax.fori_loop(0, subs, temporal, 0)

        sums = none
        for k in range(subs):
            for d in range(nsh):
                return_copy(n, k, d).wait()
            if n < STEPS - 1:
                for j in range(nsh):
                    sums = fold(sums, F[n + 1, pl.ds(j * part + k * sub, sub), :].astype(F32))
        for k in range(subs):
            for d in range(1, nsh):
                gather_copy(n, k, d).wait_send()


def solution(mesh):
    nsh, nsec = mesh.shape["shard"], mesh.shape["section"]

    def per_device(features, timesteps, conv_first, conv_second, time_weight, qkv_weight,
                   attn_out, geglu_in, geglu_out):
        _, _, rows, width, chans = features.shape
        inner = geglu_out.shape[1]
        tokens = rows * width
        part = tokens // nsh
        rim = (rows + 2) * width
        subs = min(SUBS, part // 16)
        dims = (rows, width, chans, inner, nsh, nsec, subs)
        sub = part // subs
        crowd = nsh * sub
        any_ = pl.BlockSpec(memory_space=pl.ANY)
        V = pltpu.VMEM
        D = pltpu.SemaphoreType.DMA
        scratch = [
            V((STEPS, tokens, chans), BF16),
            V((tokens, chans), BF16),
            V((2, 8, chans), F32),
            V((STEPS, tokens, chans), F32),
            V((rim + 2 * PAD, chans), F32),
            V((rim, 3 * chans), BF16),
            V((STEPS, subs, nsh, sub, chans), BF16),
            V((STEPS, subs, nsh, sub, chans), BF16),
            V((STEPS, subs, nsh, sub, chans), BF16),
            V((2 * STEPS, 8, chans), F32),
            V((2 * STEPS, 8, chans), F32),
            V((STEPS, width, chans), BF16),
            V((STEPS, width, chans), F32),
            V((STEPS, 16, chans), F32),
            V((chans, chans), F32),
            V((chans, 128), BF16),
            V((128, chans), BF16),
            V((crowd, chans), BF16),
            V((crowd, chans), F32), V((crowd, chans), F32), V((crowd, chans), F32),
            V((nsh * crowd, chans), BF16), V((nsh * crowd, chans), BF16),
            V((crowd, chans), BF16), V((crowd, chans), BF16), V((crowd, inner), BF16),
            V((3, 3 * chans, chans), BF16), V((3, 3 * chans, chans), BF16),
            V((chans, chans), BF16), V((chans, 3 * chans), BF16), V((chans, chans), BF16),
            V((chans, 2 * inner), BF16), V((chans, inner), BF16),
            D((8,)), D((SHIFTS,)), D((SHIFTS,)), D((3,)), D((3,)), D((2 * STEPS, 2)), D((2 * STEPS, 2)),
            D((STEPS, subs, nsh)), D((STEPS, subs, nsh)), D((STEPS, subs, nsh)), D((STEPS, subs, nsh)),
            D((STEPS, subs)),
        ]
        result = pl.pallas_call(
            functools.partial(kernel, dims),
            out_shape=jax.ShapeDtypeStruct((tokens, chans), BF16),
            in_specs=[pl.BlockSpec(memory_space=pltpu.SMEM)] + [any_] * 8,
            out_specs=any_,
            scratch_shapes=scratch,
            compiler_params=pltpu.CompilerParams(
                collective_id=0, has_side_effects=True, vmem_limit_bytes=60 * 1024 * 1024
            ),
        )(
            timesteps,
            features.reshape(tokens, chans),
            conv_first.reshape(3, 3 * chans, chans),
            conv_second.reshape(3, 3 * chans, chans),
            time_weight[0], qkv_weight[0], attn_out[0], geglu_in[0], jnp.swapaxes(geglu_out[0], 0, 1),
        )
        return result.reshape(features.shape)

    return jax.shard_map(
        per_device,
        mesh=mesh,
        in_specs=(
            P(("groups", "section"), "shard", "halo", None, None),
            P(("groups", "section"), None),
            P("section", None, None, None, None),
            P("section", None, None, None, None),
            P("section", None, None),
            P("section", None, None),
            P("section", None, None),
            P("section", None, None),
            P("section", None, None),
        ),
        out_specs=P(("groups", "section"), "shard", "halo", None, None),
        check_vma=False,
    )
```

profile of v0, /device:TPU:0, one launch (start us, length us, event | category | flops | bytes accessed | tf_op | source)
XLA Modules:
  0.0 73.7 jit_solution(12166551807475792505)
XLA Ops:
  0.0 71.9 %shard_map.91 = bf16[512,320]{1,0:T(8,128)(2,1)} custom-call(s32[1,2]{1,0:T(1,128)} %stamps.1, bf16[512,320]{1,0:T(8,128)(2,1)} %bitcast.17, bf16[3,960,320]{2,1,0:T(8,128)(2,1)} %bitcast.11, bf16[3,960,320]{2,1,0:T(8,128)(2,1)} %bitcast.12, bf16[320,320]{1,0:T(8,128)(2,1)} %bitcast.18, bf16[320,960]{1,0:T(8,128)(2,1)} %bitcast.16, ...), custom_call_target="tpu_custom_call" | custom-call | tf_op jit(solution)/shard_map/pallas_call | solution.py:399
  72.0 1.8 %copy.11 = bf16[1,1,8,64,320]{4,3,2,1,0:T(8,128)(2,1)} copy(bf16[1,1,8,64,320]{4,3,2,1,0:T(8,128)(2,1)} %bitcast.14) | data formatting | bytes 655360
where the time goes:
time: 73.9 us; the launch traced here: 73.7 us
  Pallas kernels  71.9 us (97%)
  local copies, waits for them, and re-layouts  1.78 us (2%)
    pallas_call x1, Pallas kernels, per_device(): pl.pallas_call(functools.partial(kernel, dims), out_shape=jax.ShapeDtypeS...  71.9 us
    unnamed x1, local copies, waits for them, and re-layouts  1.78 us

commit v1 on v0

--- a/solution.py
+++ b/solution.py
@@ -350,21 +350,510 @@
                 gather_copy(n, k, d).wait_send()
 
 
+def slab_kernel(dims, stamps, feat, cf_h, cs_h, tw_h, qkv_h, ao_h, gi_h, go_h, out, *scratch):
+    (rows, width, chans, inner, nsh, nsec, nha) = dims
+    (FX, X, EX, H, HB, EH, GM, RM, S, S2, O, SI, ST_tx, ST_rx, S0, SC, SD, emb, gmask, hmask, hmask_t,
+     N, Q, K, V, PH, PL, OB, FN, ACT, WC1, WC2, WN1, WN2, tw, qkv, ao, gi, go,
+     w_sem, c_sem, init_send, init_recv, s0_send, s0_recv, st_send, st_recv, hx_send, hx_recv, hh_send, hh_recv,
+     x_send, x_recv, out_send, out_recv, own_sem) = scratch
+    R = nsh * nha
+    q = rows // nsh
+    T = q * width
+    NF = nsh
+    CH = 2 if NF % 2 == 0 else 1
+    sub = T // 2
+    crowd = NF * sub
+    main = chans // 256 * 256
+    rest = chans - main
+    deep = 3 * main
+    me = lax.axis_index("shard")
+    sec = lax.axis_index("section")
+    side = lax.axis_index("halo")
+    r = me * nha + side
+    nxt = lax.rem(sec + 1, nsec)
+    has_up = r > 0
+    has_down = r < R - 1
+
+    own = pltpu.make_async_copy(feat, FX, w_sem.at[0])
+    own.start()
+
+    def peer(rr, section):
+        return {"shard": lax.div(rr, nha), "halo": lax.rem(rr, nha), "section": section}
+
+    barrier = pltpu.get_barrier_semaphore()
+    peers = [peer(lax.rem(r + d, R), sec) for d in range(1, R)]
+    for e in sorted({1 % nsec, (nsec - 1) % nsec} - {0}):
+        for d in range(R):
+            peers.append(peer(lax.rem(r + d, R), lax.rem(sec + e, nsec)))
+    for p in peers:
+        pl.semaphore_signal(barrier, inc=1, device_id=p, device_id_type=MESH)
+
+    loads = [
+        pltpu.make_async_copy(src, dst, w_sem.at[1 + i])
+        for i, (src, dst) in enumerate(((tw_h, tw), (qkv_h, qkv), (ao_h, ao), (gi_h, gi), (go_h, go)))
+    ]
+
+    def conv_loads(src, dst, k):
+        copies = []
+        for t in range(3):
+            copies.append(pltpu.make_async_copy(
+                src.at[t, :, pl.ds(0, main), :], dst.at[:, pl.ds(t * main, main), :], c_sem.at[k, 2 * t]))
+            copies.append(pltpu.make_async_copy(
+                src.at[t, :, pl.ds(main, rest), :], dst.at[:, pl.ds(deep + t * rest, rest), :], c_sem.at[k, 2 * t + 1]))
+        return copies
+
+    first_loads = conv_loads(cf_h, WC1, 0)
+    second_loads = conv_loads(cs_h, WC2, 1)
+    loads[0].start()
+    for c in first_loads + second_loads:
+        c.start()
+    for c in loads[1:]:
+        c.start()
+    pl.semaphore_wait(barrier, len(peers))
+
+    def remote(src, dst, send, recv, device):
+        return pltpu.make_async_remote_copy(
+            src_ref=src, dst_ref=dst, send_sem=send, recv_sem=recv, device_id=device, device_id_type=MESH)
+
+    def init_copy(j):
+        return remote(feat.at[pl.ds(j * T, T)], X.at[0, me], init_send.at[j], init_recv.at[me],
+                      peer(side * nsh + j, nxt))
+
+    def init_wait(f):
+        return remote(feat.at[pl.ds(0, T)], X.at[0, f], init_send.at[0], init_recv.at[f], peer(r, nxt))
+
+    for j in range(nsh):
+        init_copy(j).start()
+
+    def start_sums(v):
+        v = v.reshape(v.shape[0] // 8, 8, v.shape[1])
+        return jnp.sum(v, axis=0), jnp.sum(v * v, axis=0)
+
+    own.wait()
+    none = jnp.zeros((8, chans), F32)
+
+    def own_total(i, carry):
+        s1, s2 = start_sums(FX[pl.ds(pl.multiple_of(i * BLK, BLK), BLK), :].astype(F32))
+        return carry[0] + s1, carry[1] + s2
+    s1, s2 = lax.fori_loop(0, rows * width // BLK, own_total, (none, none), unroll=UNROLL)
+    S0[0:1, :] = jnp.sum(s1, axis=0, keepdims=True)
+    S0[1:2, :] = jnp.sum(s2, axis=0, keepdims=True)
+
+    def s0_copy(d):
+        return remote(S0, SI.at[me, side], s0_send.at[d], s0_recv.at[me, side], peer(lax.rem(r + d, R), nxt))
+
+    def s0_wait(f, h):
+        return remote(S0, SI.at[f, h], s0_send.at[0], s0_recv.at[f, h], peer(r, nxt))
+
+    for d in range(R):
+        s0_copy(d).start()
+
+    per = chans // GROUPS
+    ci = lax.broadcasted_iota(jnp.int32, (chans, chans), 0)
+    cj = lax.broadcasted_iota(jnp.int32, (chans, chans), 1)
+    gmask[...] = jnp.where(ci - lax.rem(ci, per) == cj - lax.rem(cj, per), 1.0, 0.0).astype(BF16)
+    lanes = hmask.shape[1]
+    hi_ = lax.broadcasted_iota(jnp.int32, (chans, lanes), 0)
+    hj_ = lax.broadcasted_iota(jnp.int32, (chans, lanes), 1)
+    hmask[...] = jnp.where(hi_ - lax.rem(hi_, HEAD_DIM) == hj_ * HEAD_DIM, HEAD_DIM ** (-0.5), 0.0).astype(BF16)
+    ti_ = lax.broadcasted_iota(jnp.int32, (lanes, chans), 0)
+    tj_ = lax.broadcasted_iota(jnp.int32, (lanes, chans), 1)
+    hmask_t[...] = jnp.where(tj_ - lax.rem(tj_, HEAD_DIM) == ti_ * HEAD_DIM, 1.0, 0.0).astype(BF16)
+    SC[...] = jnp.zeros_like(SC)
+
+    loads[0].wait()
+    half = chans // 2
+    lane = lax.broadcasted_iota(jnp.int32, (16, chans), 1)
+    k_of = jnp.where(lane < half, lane, lane - half).astype(F32)
+    frequency = jnp.exp(-math.log(10000.0) * k_of / half)
+    for n in range(STEPS):
+        angles = stamps[0, n].astype(F32) * frequency
+        wave = jnp.where(lane < half, jnp.cos(angles), jnp.sin(angles))
+        emb[n] = matmul(silu(wave).astype(BF16), tw[...])
+
+    def pack(WC, WN):
+        WN[:, 0:rest] = WC[0, :, main:]
+        WN[:, rest:2 * rest] = WC[2, :, main:]
+        WN[:, 2 * rest:3 * rest] = WC[1, :, main:]
+        WN[:, 3 * rest:] = jnp.zeros((3 * chans, WN.shape[1] - 3 * rest), BF16)
+
+    for c in first_loads:
+        c.wait()
+    pack(WC1, WN1)
+    for c in second_loads:
+        c.wait()
+    pack(WC2, WN2)
+
+    count = float(rows * nha * width * per)
+
+    def stat_copy(slot, f, d, section):
+        return remote(ST_tx.at[slot, f], ST_rx.at[slot, f, d], st_send.at[slot, f, d], st_recv.at[slot, f, d],
+                      peer(lax.rem(r + d, R), section))
+
+    def edge_x(n, f, way):
+        src = X.at[n, f, pl.ds(way * (T - width), width)]
+        return remote(src, EX.at[n, 1 - way, f], hx_send.at[n, way, f], hx_recv.at[n, 1 - way, f],
+                      peer(jnp.clip(r + 2 * way - 1, 0, R - 1), sec))
+
+    def edge_h(n, c, way):
+        span = pl.ds(c * CH, CH)
+        return remote(HB.at[n, way, span], EH.at[n, 1 - way, span], hh_send.at[n, way, c], hh_recv.at[n, 1 - way, c],
+                      peer(jnp.clip(r + 2 * way - 1, 0, R - 1), sec))
+
+    def on_edges(act, up, down):
+        @pl.when(has_up)
+        def _():
+            act(up)
+
+        @pl.when(has_down)
+        def _():
+            act(down)
+
+    def start(copies):
+        for c in copies:
+            c.start()
+
+    def wait_recv(copies):
+        for c in copies:
+            c.wait_recv()
+
+    def wait_send(copies):
+        for c in copies:
+            c.wait_send()
+
+    def scales(totals):
+        for i, tot in enumerate(totals):
+            high = tot.astype(BF16).astype(F32)
+            left = tot - high
+            mid = left.astype(BF16).astype(F32)
+            for p, v in enumerate((high, mid, left - mid)):
+                SC[2 * (p * CH + i):2 * (p * CH + i) + 2, :] = v
+        SD[...] = matmul(SC[...].astype(BF16), gmask[...])
+        got = []
+        for i in range(CH):
+            def row(j, i=i):
+                return sum(SD[2 * (p * CH + i) + j:2 * (p * CH + i) + j + 1, :] for p in range(3)) / count
+            average, second = row(0), row(1)
+            got.append((average, 0.5 * lax.rsqrt(second - average * average + 1e-05)))
+        return got
+
+    def glow(v, average, slope):
+        u = (v - average) * slope
+        return u + u * jnp.tanh(u)
+
+    up_big = jnp.full((width, main), r, jnp.int32)
+    up_small = jnp.full((width, rest), r, jnp.int32)
+
+    def activate(f, load, average, slope):
+        tails = []
+        for i in range(q + 2):
+            big = glow(load(i, 0, main), average[:, :main], slope[:, :main])
+            small = glow(load(i, main, rest), average[:, main:], slope[:, main:])
+            if i == 0:
+                big = jnp.where(up_big > 0, big, 0.0)
+                small = jnp.where(up_small > 0, small, 0.0)
+            if i == q + 1:
+                big = jnp.where(up_big < R - 1, big, 0.0)
+                small = jnp.where(up_small < R - 1, small, 0.0)
+            GM[f, pl.ds(i * width, width), :] = big.astype(BF16)
+            tails.append(small.astype(BF16))
+        for o in range(q):
+            for t in range(3):
+                RM[f, pl.ds(o * width, width), t * rest:(t + 1) * rest] = tails[o + t]
+
+    def conv(WC, WN, c):
+        size = CH * T
+        lhs = jnp.concatenate([
+            jnp.concatenate([GM[f, pl.ds(t * width, T), :] for t in range(3)] + [RM[f]], axis=1)
+            for f in range(c * CH, (c + 1) * CH)
+        ], axis=0)
+        col = lax.rem(lax.broadcasted_iota(jnp.int32, (size, main), 0), width)
+        left = jnp.where(col == 0, 0.0, pltpu.roll(matmul(lhs, WC[0, :, 0:main]), 1, 0))
+        right = jnp.where(col == width - 1, 0.0, pltpu.roll(matmul(lhs, WC[2, :, 0:main]), size - 1, 0))
+        big = matmul(lhs, WC[1, :, 0:main]) + left + right
+        last = matmul(lhs, WN[...])
+        col = lax.rem(lax.broadcasted_iota(jnp.int32, last.shape, 0), width)
+        left = jnp.where(col == 0, 0.0, pltpu.roll(last, 1, 0))
+        right = jnp.where(col == width - 1, 0.0, pltpu.roll(last, size - 1, 0))
+        small = last[:, 2 * rest:3 * rest] + left[:, 0:rest] + right[:, rest:2 * rest]
+        return big, small
+
+    def put_sums(slot, f, v, a, b):
+        s1, s2 = start_sums(v)
+        ST_tx[slot, f, 0:1, a:b] = jnp.sum(s1, axis=0, keepdims=True)
+        ST_tx[slot, f, 1:2, a:b] = jnp.sum(s2, axis=0, keepdims=True)
+
+    def layer_norm(v):
+        centred = v - jnp.mean(v, axis=-1, keepdims=True)
+        spread = jnp.mean(centred * centred, axis=-1, keepdims=True)
+        return (centred * lax.rsqrt(spread + 1e-05)).astype(BF16)
+
+    def attend(k, carry):
+        at = pl.ds(pl.multiple_of(k * sub, 16), sub)
+        for f in range(NF):
+            N[f * sub:(f + 1) * sub, :] = layer_norm(S[f, at, :].astype(F32))
+        proj = matmul(N[...], qkv[...]).astype(BF16)
+        Q[...] = proj[:, :chans].astype(F32)
+        K[...] = proj[:, chans:2 * chans].astype(F32)
+        V[...] = proj[:, 2 * chans:].astype(F32)
+
+        def frame(f, c):
+            qf = Q[pl.ds(pl.multiple_of(f * sub, 16), sub), :]
+            base = pl.multiple_of(f * crowd, 16)
+            for g in range(NF):
+                prod = qf * K[g * sub:(g + 1) * sub, :]
+                high = prod.astype(BF16)
+                PH[pl.ds(base + g * sub, sub), :] = high
+                PL[pl.ds(base + g * sub, sub), :] = (prod - high.astype(F32)).astype(BF16)
+            score = matmul(PH[pl.ds(base, crowd), :], hmask[...]) + matmul(PL[pl.ds(base, crowd), :], hmask[...])
+            pieces = [score[g * sub:(g + 1) * sub] for g in range(NF)]
+            top = functools.reduce(jnp.maximum, pieces)
+            pieces = [jnp.exp(p - top) for p in pieces]
+            scale = 1.0 / functools.reduce(jnp.add, pieces)
+            weights = jnp.concatenate([(p * scale).astype(BF16) for p in pieces], axis=0)
+            weights = matmul(weights, hmask_t[...])
+            mixed = weights[0:sub] * V[0:sub, :]
+            for g in range(1, NF):
+                mixed = mixed + weights[g * sub:(g + 1) * sub] * V[g * sub:(g + 1) * sub, :]
+            OB[pl.ds(pl.multiple_of(f * sub, 16), sub), :] = mixed.astype(BF16)
+            return c
+        lax.fori_loop(0, NF, frame, 0, unroll=NF)
+        mixed = matmul(OB[...], ao[...])
+        for f in range(NF):
+            S2[f, at, :] = (mixed[f * sub:(f + 1) * sub] + S[f, at, :].astype(F32)).astype(BF16)
+        return carry
+
+    def feed(n, f):
+        FN[...] = layer_norm(S2[f].astype(F32))
+        wide = 256
+        for j in range(inner // wide):
+            value = matmul(FN[...], gi[:, j * wide:(j + 1) * wide])
+            gate = matmul(FN[...], gi[:, inner + j * wide:inner + (j + 1) * wide])
+            gelu = 0.5 * gate * (1.0 + lax.erf(gate * (0.5 ** 0.5)))
+            ACT[:, j * wide:(j + 1) * wide] = (value * gelu).astype(BF16)
+        made = (matmul_t(ACT[...], go[...]) + S2[f].astype(F32)).astype(BF16)
+        O[n, f] = made
+        return made
+
+    def x_copy(f):
+        return remote(O.at[0, f], X.at[1, f], x_send.at[f], x_recv.at[f], peer(r, nxt))
+
+    target = lax.div(r, nsh)
+    piece = lax.rem(r, nsh)
+
+    def out_copy(f):
+        return remote(O.at[STEPS - 1, f], out.at[pl.ds(pl.multiple_of(piece * T, 16), T)],
+                      out_send.at[f], out_recv.at[piece], {"shard": f, "halo": target})
+
+    def out_local(f):
+        return pltpu.make_async_copy(O.at[STEPS - 1, f], out.at[pl.ds(pl.multiple_of(piece * T, 16), T)], own_sem)
+
+    def is_own(f):
+        return jnp.logical_and(f == me, target == side)
+
+    for n in range(STEPS):
+        for f in range(NF):
+            if n == 0:
+                init_wait(f).wait_recv()
+            else:
+                x_copy(f).wait_recv()
+            on_edges(start, [edge_x(n, f, 0)], [edge_x(n, f, 1)])
+
+        for c in range(NF // CH):
+            frames = range(c * CH, (c + 1) * CH)
+            totals = []
+            for f in frames:
+                if n == 0:
+                    for h in range(nha):
+                        s0_wait(f, h).wait_recv()
+                    totals.append(functools.reduce(jnp.add, [SI[f, h] for h in range(nha)]))
+                else:
+                    for d in range(R):
+                        stat_copy(1, f, d, nxt).wait_recv()
+                    totals.append(functools.reduce(jnp.add, [ST_rx[1, f, d] for d in range(R)]))
+            found = scales(totals)
+            on_edges(wait_recv, [edge_x(n, f, 1) for f in frames], [edge_x(n, f, 0) for f in frames])
+            for f, (average, slope) in zip(frames, found):
+                def load(i, a, size, f=f):
+                    if 0 < i <= q:
+                        return X[n, f, pl.ds((i - 1) * width, width), a:a + size].astype(F32)
+                    return EX[n, 0 if i == 0 else 1, f, :, a:a + size].astype(F32)
+                activate(f, load, average, slope)
+            big, small = conv(WC1, WN1, c)
+            big = big + emb[n, 0:1, 0:main]
+            small = small + emb[n, 0:1, main:]
+            slot = 0 if n == 0 else 2
+            for i, f in enumerate(frames):
+                for v, a, b in ((big[i * T:(i + 1) * T], 0, main), (small[i * T:(i + 1) * T], main, chans)):
+                    H[f, :, a:b] = v
+                    HB[n, 0, f, :, a:b] = v[0:width].astype(BF16)
+                    HB[n, 1, f, :, a:b] = v[T - width:].astype(BF16)
+                    put_sums(slot, f, v, a, b)
+            on_edges(start, [edge_h(n, c, 0)], [edge_h(n, c, 1)])
+            for f in frames:
+                for d in range(1, R):
+                    stat_copy(slot, f, d, sec).start()
+
+        for c in range(NF // CH):
+            frames = range(c * CH, (c + 1) * CH)
+            totals = []
+            for f in frames:
+                for d in range(1, R):
+                    stat_copy(slot, f, d, sec).wait_recv()
+                totals.append(functools.reduce(
+                    jnp.add, [ST_tx[slot, f]] + [ST_rx[slot, f, d] for d in range(1, R)]))
+            found = scales(totals)
+            on_edges(wait_recv, [edge_h(n, c, 1)], [edge_h(n, c, 0)])
+            for f, (average, slope) in zip(frames, found):
+                def load(i, a, size, f=f):
+                    if 0 < i <= q:
+                        return H[f, pl.ds((i - 1) * width, width), a:a + size]
+                    return EH[n, 0 if i == 0 else 1, f, :, a:a + size].astype(F32)
+                activate(f, load, average, slope)
+            big, small = conv(WC2, WN2, c)
+            for i, f in enumerate(frames):
+                for v, a, b in ((big[i * T:(i + 1) * T], 0, main), (small[i * T:(i + 1) * T], main, chans)):
+                    S[f, :, a:b] = (v + X[n, f, :, a:b].astype(F32)).astype(BF16)
+
+        if n == 0:
+            for load in loads[1:]:
+                load.wait()
+        lax.fori_loop(0, T // sub, attend, 0)
+
+        if n < STEPS - 1:
+            def pass_on(f, carry):
+                made = feed(0, f).astype(F32)
+                x_copy(f).start()
+                put_sums(1, f, made, 0, chans)
+                for d in range(R):
+                    stat_copy(1, f, d, nxt).start()
+                return carry
+            lax.fori_loop(0, NF, pass_on, 0)
+        else:
+            def hand_in(k, carry):
+                f = lax.rem(me + 1 + k, NF)
+                feed(STEPS - 1, f)
+
+                @pl.when(is_own(f))
+                def _():
+                    out_local(f).start()
+
+                @pl.when(jnp.logical_not(is_own(f)))
+                def _():
+                    out_copy(f).start()
+                return carry
+            lax.fori_loop(0, NF, hand_in, 0)
+
+    for j in range(nsh):
+        init_copy(j).wait_send()
+    for d in range(R):
+        s0_copy(d).wait_send()
+    for n in range(STEPS):
+        on_edges(wait_send, [edge_x(n, f, 0) for f in range(NF)], [edge_x(n, f, 1) for f in range(NF)])
+        on_edges(wait_send, [edge_h(n, c, 0) for c in range(NF // CH)], [edge_h(n, c, 1) for c in range(NF // CH)])
+    for f in range(NF):
+        for d in range(1, R):
+            stat_copy(0, f, d, sec).wait_send()
+            stat_copy(2, f, d, sec).wait_send()
+        for d in range(R):
+            stat_copy(1, f, d, nxt).wait_send()
+        x_copy(f).wait_send()
+
+    for f in range(NF):
+        @pl.when(is_own(f))
+        def _():
+            out_local(f).wait()
+
+        @pl.when(jnp.logical_not(is_own(f)))
+        def _():
+            out_copy(f).wait_send()
+    for j in range(nsh):
+        @pl.when(side * nsh + j != r)
+        def _():
+            remote(O.at[STEPS - 1, 0], out.at[pl.ds(j * T, T)], out_send.at[0], out_recv.at[j],
+                   {"halo": 1 - side}).wait_recv()
+
+
+def slab_scratch(rows, width, chans, inner, nsh, nha):
+    V = pltpu.VMEM
+    D = pltpu.SemaphoreType.DMA
+    R = nsh * nha
+    q = rows // nsh
+    T = q * width
+    NF = nsh
+    CH = 2 if NF % 2 == 0 else 1
+    crowd = NF * (T // 2)
+    main = chans // 256 * 256
+    rest = chans - main
+    return [
+        V((rows * width, chans), BF16),
+        V((STEPS, NF, T, chans), BF16),
+        V((STEPS, 2, NF, width, chans), BF16),
+        V((NF, T, chans), F32),
+        V((STEPS, 2, NF, width, chans), BF16),
+        V((STEPS, 2, NF, width, chans), BF16),
+        V((NF, (q + 2) * width, main), BF16),
+        V((NF, T, 3 * rest), BF16),
+        V((NF, T, chans), BF16),
+        V((NF, T, chans), BF16),
+        V((STEPS, NF, T, chans), BF16),
+        V((NF, nha, 2, chans), F32),
+        V((3, NF, 2, chans), F32),
+        V((3, NF, R, 2, chans), F32),
+        V((2, chans), F32),
+        V((16, chans), F32),
+        V((16, chans), F32),
+        V((STEPS, 16, chans), F32),
+        V((chans, chans), BF16),
+        V((chans, 128), BF16),
+        V((128, chans), BF16),
+        V((crowd, chans), BF16),
+        V((crowd, chans), F32), V((crowd, chans), F32), V((crowd, chans), F32),
+        V((NF * crowd, chans), BF16), V((NF * crowd, chans), BF16),
+        V((crowd, chans), BF16), V((T, chans), BF16), V((T, inner), BF16),
+        V((3, 3 * chans, chans), BF16), V((3, 3 * chans, chans), BF16),
+        V((3 * chans, -(-3 * rest // 128) * 128), BF16), V((3 * chans, -(-3 * rest // 128) * 128), BF16),
+        V((chans, chans), BF16), V((chans, 3 * chans), BF16), V((chans, chans), BF16),
+        V((chans, 2 * inner), BF16), V((chans, inner), BF16),
+        D((6,)), D((2, 6)), D((nsh,)), D((NF,)), D((R,)), D((NF, nha)), D((3, NF, R)), D((3, NF, R)),
+        D((STEPS, 2, NF)), D((STEPS, 2, NF)), D((STEPS, 2, NF // CH)), D((STEPS, 2, NF // CH)),
+        D((NF,)), D((NF,)), D((NF,)), D((nsh,)), D(()),
+    ]
+
+
 def solution(mesh):
-    nsh, nsec = mesh.shape["shard"], mesh.shape["section"]
+    nsh, nsec, nha = mesh.shape["shard"], mesh.shape["section"], mesh.shape["halo"]
 
     def per_device(features, timesteps, conv_first, conv_second, time_weight, qkv_weight,
                    attn_out, geglu_in, geglu_out):
         _, _, rows, width, chans = features.shape
         inner = geglu_out.shape[1]
         tokens = rows * width
+        any_ = pl.BlockSpec(memory_space=pl.ANY)
+        if nsec > 1 and nha == 2 and rows % nsh == 0 and chans > 256 and chans % 256 and rows // nsh * width % 32 == 0:
+            result = pl.pallas_call(
+                functools.partial(slab_kernel, (rows, width, chans, inner, nsh, nsec, nha)),
+                out_shape=jax.ShapeDtypeStruct((tokens, chans), BF16),
+                in_specs=[pl.BlockSpec(memory_space=pltpu.SMEM)] + [any_] * 8,
+                out_specs=any_,
+                scratch_shapes=slab_scratch(rows, width, chans, inner, nsh, nha),
+                compiler_params=pltpu.CompilerParams(
+                    collective_id=0, has_side_effects=True, vmem_limit_bytes=60 * 1024 * 1024
+                ),
+            )(
+                timesteps,
+                features.reshape(tokens, chans),
+                conv_first.reshape(3, 3, chans, chans),
+                conv_second.reshape(3, 3, chans, chans),
+                time_weight[0], qkv_weight[0], attn_out[0], geglu_in[0], jnp.swapaxes(geglu_out[0], 0, 1),
+            )
+            return result.reshape(features.shape)
         part = tokens // nsh
         rim = (rows + 2) * width
         subs = min(SUBS, part // 16)
         dims = (rows, width, chans, inner, nsh, nsec, subs)
         sub = part // subs
         crowd = nsh * sub
-        any_ = pl.BlockSpec(memory_space=pl.ANY)
         V = pltpu.VMEM
         D = pltpu.SemaphoreType.DMA
         scratch = [

time: 73.9 us -> 75.8 us (1.026); the launches traced: 73.7 us -> 74.5 us
  Pallas kernels: 71.9 us -> 72.7 us
    pallas_call x1, Pallas kernels: 71.9 us -> 72.7 us  [per_device(): pl.pallas_call(functools.partial(slab_kernel, (rows, width, chans, inner,...]
where the time goes in v1:
time: 75.8 us; the launch traced here: 74.5 us
  Pallas kernels  72.7 us (96%)
  local copies, waits for them, and re-layouts  1.78 us (2%)
    pallas_call x1, Pallas kernels, per_device(): pl.pallas_call(functools.partial(slab_kernel, (rows, width, chans, inner,...  72.7 us
    unnamed x1, local copies, waits for them, and re-layouts  1.78 us

profile of v1, /device:TPU:0, one launch (start us, length us, event | category | flops | bytes accessed | tf_op | source)
XLA Modules:
  0.0 74.5 jit_solution(3770768606417047263)
XLA Ops:
  0.0 72.7 %shard_map.91 = bf16[512,320]{1,0:T(8,128)(2,1)} custom-call(s32[1,2]{1,0:T(1,128)} %stamps.1, bf16[512,320]{1,0:T(8,128)(2,1)} %bitcast.17, bf16[3,3,320,320]{3,2,1,0:T(8,128)(2,1)} %bitcast.11, bf16[3,3,320,320]{3,2,1,0:T(8,128)(2,1)} %bitcast.12, bf16[320,320]{1,0:T(8,128)(2,1)} %bitcast.18, bf16[320,960]{1,0:T(8,128)(2,1)} %bitcast.16, ...), custom_call_target="tpu_custom_call" | custom-call | tf_op jit(solution)/shard_map/pallas_call | solution.py:834
  72.7 1.8 %copy.11 = bf16[1,1,8,64,320]{4,3,2,1,0:T(8,128)(2,1)} copy(bf16[1,1,8,64,320]{4,3,2,1,0:T(8,128)(2,1)} %bitcast.14) | data formatting | bytes 655360

commit v2 on v0

--- a/solution.py
+++ b/solution.py
@@ -18,7 +18,6 @@
 SUBS = 2
 UNROLL = 4
 SHIFTS = 4
-PAD = 8
 
 
 def matmul(a, b):
@@ -35,10 +34,10 @@
 
 def kernel(dims, stamps, feat, cf_h, cs_h, tw_h, qkv_h, ao_h, gi_h, go_h, out, *scratch):
     (rows, width, chans, inner, nsh, nsec, subs) = dims
-    (F, FX, first_rx, H, G, A, S, PB, O, stat_tx, stat_rx, edge_x, edge_h, emb, gmask, hmask, hmask_t,
+    (F, FX, first_rx, H, GM, RM, SC, SD, S, PB, O, stat_tx, stat_rx, edge_x, edge_h, emb, gmask, hmask, hmask_t,
      N, Q, K, V, PH, PL, OB, S2, ACT,
-     cf, cs, tw, qkv, ao, gi, go,
-     w_sem, x_send, x_recv, first_send, first_recv, halo_send, halo_recv, in_send, in_recv, out_send, out_recv, own_sem) = scratch
+     cf, cs, cf_n, cs_n, tw, qkv, ao, gi, go,
+     w_sem, c_sem, x_send, x_recv, first_send, first_recv, halo_send, halo_recv, in_send, in_recv, out_send, out_recv, own_sem) = scratch
     tokens = rows * width
     part = tokens // nsh
     sub = part // subs
@@ -49,15 +48,30 @@
     side = lax.axis_index("halo")
     nxt = lax.rem(sec + 1, nsec)
 
+    main = chans // 256 * 256
+    rest = chans - main
     own = pltpu.make_async_copy(feat, FX, w_sem.at[7])
     own.start()
     loads = [
         pltpu.make_async_copy(src, dst, w_sem.at[i])
         for i, (src, dst) in enumerate(
-            ((cf_h, cf), (cs_h, cs), (tw_h, tw), (qkv_h, qkv), (ao_h, ao), (gi_h, gi), (go_h, go))
+            ((tw_h, tw), (qkv_h, qkv), (ao_h, ao), (gi_h, gi), (go_h, go))
         )
     ]
-    for load in loads:
+
+    def conv_loads(src, dst, k):
+        copies = []
+        for t in range(3):
+            copies.append(pltpu.make_async_copy(
+                src.at[t, :, pl.ds(0, main), :], dst.at[:, pl.ds(t * main, main), :], c_sem.at[k, 2 * t]))
+            copies.append(pltpu.make_async_copy(
+                src.at[t, :, pl.ds(main, rest), :], dst.at[:, pl.ds(3 * main + t * rest, rest), :],
+                c_sem.at[k, 2 * t + 1]))
+        return copies
+
+    first_loads = conv_loads(cf_h, cf, 0)
+    second_loads = conv_loads(cs_h, cs, 1)
+    for load in [loads[0]] + first_loads + second_loads + loads[1:]:
         load.start()
 
     def at(shard, section):
@@ -103,14 +117,14 @@
 
     def fold(carry, v):
         s1, s2 = carry
-        v = v.reshape(v.shape[0] // 8, 8, chans)
+        v = v.reshape(v.shape[0] // 8, 8, v.shape[1])
         return s1 + jnp.sum(v, axis=0), s2 + jnp.sum(v * v, axis=0)
 
     none = (jnp.zeros((8, chans), F32), jnp.zeros((8, chans), F32))
 
-    def publish(slot, sums):
-        stat_tx[slot, 0:1, :] = jnp.sum(sums[0], axis=0, keepdims=True)
-        stat_tx[slot, 1:2, :] = jnp.sum(sums[1], axis=0, keepdims=True)
+    def publish(slot, sums, a=0, b=chans):
+        stat_tx[slot, 0:1, a:b] = jnp.sum(sums[0], axis=0, keepdims=True)
+        stat_tx[slot, 1:2, a:b] = jnp.sum(sums[1], axis=0, keepdims=True)
 
     own.wait()
 
@@ -125,7 +139,7 @@
     per = chans // GROUPS
     ci = lax.broadcasted_iota(jnp.int32, (chans, chans), 0)
     cj = lax.broadcasted_iota(jnp.int32, (chans, chans), 1)
-    gmask[...] = jnp.where(ci - lax.rem(ci, per) == cj - lax.rem(cj, per), 1.0, 0.0).astype(F32)
+    gmask[...] = jnp.where(ci - lax.rem(ci, per) == cj - lax.rem(cj, per), 1.0, 0.0).astype(BF16)
     lanes = hmask.shape[1]
     hi_ = lax.broadcasted_iota(jnp.int32, (chans, lanes), 0)
     hj_ = lax.broadcasted_iota(jnp.int32, (chans, lanes), 1)
@@ -133,13 +147,11 @@
     ti_ = lax.broadcasted_iota(jnp.int32, (lanes, chans), 0)
     tj_ = lax.broadcasted_iota(jnp.int32, (lanes, chans), 1)
     hmask_t[...] = jnp.where(tj_ - lax.rem(tj_, HEAD_DIM) == ti_ * HEAD_DIM, 1.0, 0.0).astype(BF16)
-    zeros_rim = jnp.zeros((width, chans), F32)
-    G[pl.ds(0, PAD), :] = jnp.zeros((PAD, chans), F32)
-    G[pl.ds(PAD + rim, PAD), :] = jnp.zeros((PAD, chans), F32)
-    G[pl.ds(PAD, width), :] = zeros_rim
-    G[pl.ds(PAD + rim - width, width), :] = zeros_rim
-
-    loads[2].wait()
+    for at_ in (0, rim - width):
+        GM[pl.ds(at_, width), :] = jnp.zeros((width, main), BF16)
+    SC[...] = jnp.zeros_like(SC)
+
+    loads[0].wait()
     half = chans // 2
     lane = lax.broadcasted_iota(jnp.int32, (16, chans), 1)
     k_of = jnp.where(lane < half, lane, lane - half).astype(F32)
@@ -149,7 +161,16 @@
         wave = jnp.where(lane < half, jnp.cos(angles), jnp.sin(angles))
         emb[n] = matmul(silu(wave).astype(BF16), tw[...])
 
-    rim_at = pl.multiple_of(PAD + (1 - side) * (rim - width), 8)
+    def pack(full, narrow):
+        narrow[:, 0:rest] = full[0, :, main:]
+        narrow[:, rest:2 * rest] = full[2, :, main:]
+        narrow[:, 2 * rest:3 * rest] = full[1, :, main:]
+        narrow[:, 3 * rest:] = jnp.zeros((3 * chans, narrow.shape[1] - 3 * rest), BF16)
+
+    for c in first_loads:
+        c.wait()
+    pack(cf, cf_n)
+    rim_at = pl.multiple_of((1 - side) * (rim - width), 16)
     count = float(rows * 2 * width * per)
 
     def swap(slot, edge_src, edge_dst):
@@ -165,41 +186,56 @@
         return copies
 
     def moments(both):
-        summed = jnp.dot(both, gmask[...], preferred_element_type=F32, precision=lax.Precision.HIGHEST)
-        average = summed[0:1, :] / count
-        second = summed[1:2, :] / count
-        return average, lax.rsqrt(second - average * average + 1e-05)
+        high = both.astype(BF16).astype(F32)
+        left = both - high
+        mid = left.astype(BF16).astype(F32)
+        for p, v in enumerate((high, mid, left - mid)):
+            SC[2 * p:2 * p + 2, :] = v[0:2]
+        SD[...] = matmul(SC[...].astype(BF16), gmask[...])
+        average = (SD[0:1, :] + SD[2:3, :] + SD[4:5, :]) / count
+        second = (SD[1:2, :] + SD[3:4, :] + SD[5:6, :]) / count
+        return average, 0.5 * lax.rsqrt(second - average * average + 1e-05)
+
+    def glow(v, average, slope):
+        u = (v - average) * slope
+        return u + u * jnp.tanh(u)
+
+    below = jnp.full((width, rest), side, jnp.int32)
 
     def activate(load, load_edge, both, arrivals=()):
-        average, inverse = moments(both)
-
-        def one(i, c):
-            at_ = pl.multiple_of(i * BLK, BLK)
-            G[pl.ds(PAD + width + at_, BLK), :] = silu((load(pl.ds(at_, BLK)) - average) * inverse)
-            return c
+        average, slope = moments(both)
         stages = max(len(arrivals), 1)
-        for i in range(stages):
-            if arrivals:
-                arrivals[i].wait_recv()
-            lax.fori_loop(i * (tokens // BLK) // stages, (i + 1) * (tokens // BLK) // stages, one, 0, unroll=2)
-        G[pl.ds(rim_at, width), :] = silu((load_edge() - average) * inverse)
-        col = lax.rem(lax.broadcasted_iota(jnp.int32, (width, chans), 0), width)
-
-        def two(i, c):
-            at_ = pl.multiple_of(i * width, width)
-            window = G[pl.ds(at_, width + 2 * PAD), :]
-            left = window[PAD - 1 : PAD - 1 + width]
-            mid = window[PAD : PAD + width]
-            right = window[PAD + 1 : PAD + 1 + width]
-            dst = pl.ds(at_, width)
-            A[dst, 0:chans] = jnp.where(col == 0, 0.0, left).astype(BF16)
-            A[dst, chans : 2 * chans] = mid.astype(BF16)
-            A[dst, 2 * chans :] = jnp.where(col == width - 1, 0.0, right).astype(BF16)
-            return c
-        lax.fori_loop(0, rows + 2, two, 0, unroll=5)
-
-    def conv(weights, start, size):
-        return sum(matmul(A[pl.ds(start + r * width, size), :], weights[r]) for r in range(3))
+        for i in range(rows):
+            if arrivals and i % (rows // stages) == 0:
+                arrivals[i // (rows // stages)].wait_recv()
+            v = load(pl.ds(i * width, width))
+            GM[pl.ds((i + 1) * width, width), :] = glow(v[:, :main], average[:, :main], slope[:, :main]).astype(BF16)
+            small = glow(v[:, main:], average[:, main:], slope[:, main:]).astype(BF16)
+            for t in range(3):
+                if 0 <= i + 1 - t < rows:
+                    RM[pl.ds((i + 1 - t) * width, width), t * rest:(t + 1) * rest] = small
+        v = load_edge()
+        GM[pl.ds(rim_at, width), :] = glow(v[:, :main], average[:, :main], slope[:, :main]).astype(BF16)
+        small = glow(v[:, main:], average[:, main:], slope[:, main:])
+        RM[pl.ds(0, width), 0:rest] = jnp.where(below > 0, small, 0.0).astype(BF16)
+        RM[pl.ds((rows - 1) * width, width), 2 * rest:3 * rest] = jnp.where(below > 0, 0.0, small).astype(BF16)
+
+    def conv(full, narrow, spans, size):
+        lhs = jnp.concatenate([
+            jnp.concatenate([GM[pl.ds(a + t * width, size), :] for t in range(3)] + [RM[pl.ds(a, size), :]], axis=1)
+            for a in spans
+        ], axis=0)
+        many = size * len(spans)
+
+        def shifted(y, by):
+            col = lax.rem(lax.broadcasted_iota(jnp.int32, y.shape, 0), width)
+            return jnp.where(col == (0 if by == 1 else width - 1), 0.0, pltpu.roll(y, by, 0))
+        big = (matmul(lhs, full[1, :, 0:main]) + shifted(matmul(lhs, full[0, :, 0:main]), 1)
+               + shifted(matmul(lhs, full[2, :, 0:main]), many - 1))
+        last = matmul(lhs, narrow[...])
+        small = (last[:, 2 * rest:3 * rest] + shifted(last, 1)[:, 0:rest]
+                 + shifted(last, many - 1)[:, rest:2 * rest])
+        return big, small
 
     def normalise(src):
         def one(i, c):
@@ -287,7 +323,6 @@
             activate(load_x, lambda: edge_x[0].astype(F32), first_rx[0] + first_rx[1], shifts)
             for c in shifts:
                 c.wait_send()
-            loads[0].wait()
         else:
             swaps = swap(2 * n, field.at[pl.ds(edge_at, width)], edge_x.at[n])
             swaps[0].start()
@@ -296,37 +331,57 @@
             for c in swaps:
                 c.wait()
             activate(load_x, lambda n=n: edge_x[n].astype(F32), stat_tx[2 * n] + stat_rx[2 * n])
-        sums = none
+        big_sums = (jnp.zeros((8, main), F32), jnp.zeros((8, main), F32))
+        small_sums = (jnp.zeros((8, rest), F32), jnp.zeros((8, rest), F32))
         for i in range(2):
             rows_ = pl.ds(i * (tokens // 2), tokens // 2)
-            h1 = conv(cf, i * (tokens // 2), tokens // 2) + emb[n, 0:1, :]
-            H[n, rows_, :] = h1
-            sums = fold(sums, h1)
+            big, small = conv(cf, cf_n, [i * (tokens // 2)], tokens // 2)
+            big = big + emb[n, 0:1, 0:main]
+            small = small + emb[n, 0:1, main:]
+            H[n, rows_, 0:main] = big
+            H[n, rows_, main:] = small
+            big_sums = fold(big_sums, big)
+            small_sums = fold(small_sums, small)
 
         slot = 2 * n + 1
         swaps = swap(slot, H.at[n, pl.ds(edge_at, width)], edge_h.at[n])
         swaps[0].start()
-        publish(slot, sums)
+        publish(slot, big_sums, 0, main)
+        publish(slot, small_sums, main, chans)
         swaps[1].start()
         for c in swaps:
             c.wait()
         activate(lambda s, n=n: H[n, s, :], lambda n=n: edge_h[n], stat_tx[slot] + stat_rx[slot])
         if n == 0:
-            loads[1].wait()
+            for c in second_loads:
+                c.wait()
+            pack(cs, cs_n)
+        whole_rows = sub % width == 0
         for k in range(subs):
-            spans = [j * part + k * sub for j in range(nsh)]
-            total = sum(
-                matmul(jnp.concatenate([A[pl.ds(r * width + a, sub), :] for a in spans], axis=0), cs[r])
-                for r in range(3)
-            )
-            base = jnp.concatenate([field[pl.ds(a, sub), :] for a in spans], axis=0)
-            S[n, k] = (total + base.astype(F32)).astype(BF16).reshape(nsh, sub, chans)
-            for d in range(1, nsh):
-                gather_copy(n, k, d).start()
-            PB[n, k, me] = S[n, k, me]
+            if whole_rows:
+                spans, size = [j * part + k * sub for j in range(nsh)], sub
+            else:
+                spans, size = [k * (tokens // subs)], tokens // subs
+            big, small = conv(cs, cs_n, spans, size)
+            for i, a in enumerate(spans):
+                for b in range(0, size, sub):
+                    at_ = a + b
+                    line = slice(i * size + b, i * size + b + sub)
+                    to, kk = at_ // part, at_ % part // sub
+                    for v, lo, hi in ((big[line], 0, main), (small[line], main, chans)):
+                        S[n, kk, to, :, lo:hi] = (v + field[pl.ds(at_, sub), lo:hi].astype(F32)).astype(BF16)
+            if whole_rows:
+                for d in range(1, nsh):
+                    gather_copy(n, k, d).start()
+                PB[n, k, me] = S[n, k, me]
+        if not whole_rows:
+            for k in range(subs):
+                for d in range(1, nsh):
+                    gather_copy(n, k, d).start()
+                PB[n, k, me] = S[n, k, me]
 
         if n == 0:
-            for i in (3, 4, 5, 6):
+            for i in (1, 2, 3, 4):
                 loads[i].wait()
 
         def temporal(k, carry, n=n):
@@ -364,6 +419,8 @@
         dims = (rows, width, chans, inner, nsh, nsec, subs)
         sub = part // subs
         crowd = nsh * sub
+        main = chans // 256 * 256
+        rest = chans - main
         any_ = pl.BlockSpec(memory_space=pl.ANY)
         V = pltpu.VMEM
         D = pltpu.SemaphoreType.DMA
@@ -372,8 +429,10 @@
             V((tokens, chans), BF16),
             V((2, 8, chans), F32),
             V((STEPS, tokens, chans), F32),
-            V((rim + 2 * PAD, chans), F32),
-            V((rim, 3 * chans), BF16),
+            V((rim, main), BF16),
+            V((tokens, 3 * rest), BF16),
+            V((16, chans), F32),
+            V((16, chans), F32),
             V((STEPS, subs, nsh, sub, chans), BF16),
             V((STEPS, subs, nsh, sub, chans), BF16),
             V((STEPS, subs, nsh, sub, chans), BF16),
@@ -382,7 +441,7 @@
             V((STEPS, width, chans), BF16),
             V((STEPS, width, chans), F32),
             V((STEPS, 16, chans), F32),
-            V((chans, chans), F32),
+            V((chans, chans), BF16),
             V((chans, 128), BF16),
             V((128, chans), BF16),
             V((crowd, chans), BF16),
@@ -390,9 +449,10 @@
             V((nsh * crowd, chans), BF16), V((nsh * crowd, chans), BF16),
             V((crowd, chans), BF16), V((crowd, chans), BF16), V((crowd, inner), BF16),
             V((3, 3 * chans, chans), BF16), V((3, 3 * chans, chans), BF16),
+            V((3 * chans, -(-3 * rest // 128) * 128), BF16), V((3 * chans, -(-3 * rest // 128) * 128), BF16),
             V((chans, chans), BF16), V((chans, 3 * chans), BF16), V((chans, chans), BF16),
             V((chans, 2 * inner), BF16), V((chans, inner), BF16),
-            D((8,)), D((SHIFTS,)), D((SHIFTS,)), D((3,)), D((3,)), D((2 * STEPS, 2)), D((2 * STEPS, 2)),
+            D((8,)), D((2, 6)), D((SHIFTS,)), D((SHIFTS,)), D((3,)), D((3,)), D((2 * STEPS, 2)), D((2 * STEPS, 2)),
             D((STEPS, subs, nsh)), D((STEPS, subs, nsh)), D((STEPS, subs, nsh)), D((STEPS, subs, nsh)),
             D((STEPS, subs)),
         ]
@@ -408,8 +468,8 @@
         )(
             timesteps,
             features.reshape(tokens, chans),
-            conv_first.reshape(3, 3 * chans, chans),
-            conv_second.reshape(3, 3 * chans, chans),
+            conv_first.reshape(3, 3, chans, chans),
+            conv_second.reshape(3, 3, chans, chans),
             time_weight[0], qkv_weight[0], attn_out[0], geglu_in[0], jnp.swapaxes(geglu_out[0], 0, 1),
         )
         return result.reshape(features.shape)

time: 73.9 us -> 69.9 us (0.946)
  Pallas kernels: 71.9 us -> 67.9 us
    pallas_call x1, Pallas kernels: 71.9 us -> 67.9 us  [per_device(): pl.pallas_call(functools.partial(kernel, dims), out_shape=jax.ShapeDtypeS...]
where the time goes in v2:
time: 69.9 us; the launch traced here: 69.7 us
  Pallas kernels  67.9 us (97%)
  local copies, waits for them, and re-layouts  1.78 us (3%)
    pallas_call x1, Pallas kernels, per_device(): pl.pallas_call(functools.partial(kernel, dims), out_shape=jax.ShapeDtypeS...  67.9 us
    unnamed x1, local copies, waits for them, and re-layouts  1.78 us

profile of v2, /device:TPU:0, one launch (start us, length us, event | category | flops | bytes accessed | tf_op | source)
XLA Modules:
  0.0 69.7 jit_solution(3803970701165720684)
XLA Ops:
  0.0 67.9 %shard_map.91 = bf16[512,320]{1,0:T(8,128)(2,1)} custom-call(s32[1,2]{1,0:T(1,128)} %stamps.1, bf16[512,320]{1,0:T(8,128)(2,1)} %bitcast.17, bf16[3,3,320,320]{3,2,1,0:T(8,128)(2,1)} %bitcast.11, bf16[3,3,320,320]{3,2,1,0:T(8,128)(2,1)} %bitcast.12, bf16[320,320]{1,0:T(8,128)(2,1)} %bitcast.18, bf16[320,960]{1,0:T(8,128)(2,1)} %bitcast.16, ...), custom_call_target="tpu_custom_call" | custom-call | tf_op jit(solution)/shard_map/pallas_call | solution.py:459
  67.9 1.8 %copy.11 = bf16[1,1,8,64,320]{4,3,2,1,0:T(8,128)(2,1)} copy(bf16[1,1,8,64,320]{4,3,2,1,0:T(8,128)(2,1)} %bitcast.14) | data formatting | bytes 655360

commit v3 on v2

--- a/solution.py
+++ b/solution.py
@@ -34,8 +34,8 @@
 
 def kernel(dims, stamps, feat, cf_h, cs_h, tw_h, qkv_h, ao_h, gi_h, go_h, out, *scratch):
     (rows, width, chans, inner, nsh, nsec, subs) = dims
-    (F, FX, first_rx, H, GM, RM, SC, SD, S, PB, O, stat_tx, stat_rx, edge_x, edge_h, emb, gmask, hmask, hmask_t,
-     N, Q, K, V, PH, PL, OB, S2, ACT,
+    (F, FX, first_rx, H, GM, RM, SC, SD, S, PB, O, stat_tx, stat_rx, edge_x, edge_h, emb, gmask, gather, spread,
+     N, Q, K, V, K4, V4, PP, W, OB, S2, ACT,
      cf, cs, cf_n, cs_n, tw, qkv, ao, gi, go,
      w_sem, c_sem, x_send, x_recv, first_send, first_recv, halo_send, halo_recv, in_send, in_recv, out_send, out_recv, own_sem) = scratch
     tokens = rows * width
@@ -140,13 +140,26 @@
     ci = lax.broadcasted_iota(jnp.int32, (chans, chans), 0)
     cj = lax.broadcasted_iota(jnp.int32, (chans, chans), 1)
     gmask[...] = jnp.where(ci - lax.rem(ci, per) == cj - lax.rem(cj, per), 1.0, 0.0).astype(BF16)
-    lanes = hmask.shape[1]
-    hi_ = lax.broadcasted_iota(jnp.int32, (chans, lanes), 0)
-    hj_ = lax.broadcasted_iota(jnp.int32, (chans, lanes), 1)
-    hmask[...] = jnp.where(hi_ - lax.rem(hi_, HEAD_DIM) == hj_ * HEAD_DIM, HEAD_DIM ** (-0.5), 0.0).astype(BF16)
-    ti_ = lax.broadcasted_iota(jnp.int32, (lanes, chans), 0)
-    tj_ = lax.broadcasted_iota(jnp.int32, (lanes, chans), 1)
-    hmask_t[...] = jnp.where(tj_ - lax.rem(tj_, HEAD_DIM) == ti_ * HEAD_DIM, 1.0, 0.0).astype(BF16)
+    lanes = gather.shape[1]
+    step = lanes // nsh
+    heads = main // HEAD_DIM
+    tall = nsh * main
+    row_ = lax.broadcasted_iota(jnp.int32, (main, lanes), 0)
+    row_ = row_ - lax.rem(row_, HEAD_DIM)
+    col_ = lax.broadcasted_iota(jnp.int32, (main, lanes), 1)
+    down = lax.broadcasted_iota(jnp.int32, (lanes, main), 0)
+    over = lax.broadcasted_iota(jnp.int32, (lanes, main), 1)
+    over = over - lax.rem(over, HEAD_DIM)
+    for g in range(nsh):
+        hit = row_ == (col_ - g * step) * HEAD_DIM
+        gather[g * main:(g + 1) * main, :] = jnp.where(hit, HEAD_DIM ** (-0.5), 0.0).astype(BF16)
+        hit = col_[0:rest] == g * step + heads
+        gather[tall + g * rest:tall + (g + 1) * rest, :] = jnp.where(hit, HEAD_DIM ** (-0.5), 0.0).astype(BF16)
+        spread[:, g * main:(g + 1) * main] = jnp.where(over == (down - g * step) * HEAD_DIM, 1.0, 0.0).astype(BF16)
+    for j in range(nsh * rest // lanes):
+        low = jnp.where(over[:, 0:lanes] < HEAD_DIM, 0, step)
+        hit = down[:, 0:lanes] - (j * lanes // rest * step + heads) == low
+        spread[:, tall + j * lanes:tall + (j + 1) * lanes] = jnp.where(hit, 1.0, 0.0).astype(BF16)
     for at_ in (0, rim - width):
         GM[pl.ds(at_, width), :] = jnp.zeros((width, main), BF16)
     SC[...] = jnp.zeros_like(SC)
@@ -279,27 +292,48 @@
         K[...] = proj[:, chans : 2 * chans].astype(F32)
         V[...] = proj[:, 2 * chans :].astype(F32)
 
-        def frame(f, c):
-            q = Q[pl.ds(pl.multiple_of(f * sub, 16), sub), :]
-            start = pl.multiple_of(f * crowd, 16)
+        for g in range(nsh):
+            K4[:, g * rest:(g + 1) * rest] = K[g * sub:(g + 1) * sub, main:]
+            V4[:, g * rest:(g + 1) * rest] = V[g * sub:(g + 1) * sub, main:]
+
+        def products(f, c):
+            at_ = pl.multiple_of(f * sub, 16)
+            q = Q[pl.ds(at_, sub), :]
+            tail = jnp.concatenate([q[:, main:]] * (lanes // rest), axis=1)
+
+            def put(v, a):
+                high = v.astype(BF16)
+                PP[pl.ds(at_, sub), a:a + v.shape[1]] = high
+                PP[pl.ds(crowd + at_, sub), a:a + v.shape[1]] = (v - high.astype(F32)).astype(BF16)
             for g in range(nsh):
-                prod = q * K[g * sub : (g + 1) * sub, :]
-                high = prod.astype(BF16)
-                PH[pl.ds(start + g * sub, sub), :] = high
-                PL[pl.ds(start + g * sub, sub), :] = (prod - high.astype(F32)).astype(BF16)
-            score = matmul(PH[pl.ds(start, crowd), :], hmask[...]) + matmul(PL[pl.ds(start, crowd), :], hmask[...])
-            pieces = [score[g * sub : (g + 1) * sub] for g in range(nsh)]
-            top = functools.reduce(jnp.maximum, pieces)
-            pieces = [jnp.exp(p - top) for p in pieces]
-            scale = 1.0 / functools.reduce(jnp.add, pieces)
-            weights = jnp.concatenate([(p * scale).astype(BF16) for p in pieces], axis=0)
-            weights = matmul(weights, hmask_t[...])
-            mixed = weights[0:sub] * V[0:sub, :]
+                put(q[:, :main] * K[g * sub:(g + 1) * sub, :main], g * main)
+            for a in range(0, nsh * rest, lanes):
+                put(tail * K4[:, a:a + lanes], tall + a)
+            return c
+        lax.fori_loop(0, nsh, products, 0, unroll=4)
+        score = matmul(PP[...], gather[...])
+        score = score[:crowd] + score[crowd:]
+
+        def across(fold_, v):
+            turn = step
+            while turn < lanes:
+                v = fold_(v, pltpu.roll(v, turn, 1))
+                turn *= 2
+            return v
+        score = jnp.exp(score - across(jnp.maximum, score))
+        W[...] = (score * (1.0 / across(jnp.add, score))).astype(BF16)
+        weights = matmul(W[...], spread[...])
+        for f in range(nsh):
+            mine = weights[f * sub:(f + 1) * sub]
+            mixed = mine[:, :main] * V[0:sub, :main]
             for g in range(1, nsh):
-                mixed = mixed + weights[g * sub : (g + 1) * sub] * V[g * sub : (g + 1) * sub, :]
-            OB[pl.ds(pl.multiple_of(f * sub, 16), sub), :] = mixed.astype(BF16)
-            return c
-        lax.fori_loop(0, nsh, frame, 0, unroll=4)
+                mixed = mixed + mine[:, g * main:(g + 1) * main] * V[g * sub:(g + 1) * sub, :main]
+            OB[f * sub:(f + 1) * sub, :main] = mixed.astype(BF16)
+            tail = mine[:, tall:tall + lanes] * V4[:, 0:lanes]
+            for a in range(lanes, nsh * rest, lanes):
+                tail = tail + mine[:, tall + a:tall + a + lanes] * V4[:, a:a + lanes]
+            tail = tail + pltpu.roll(tail, rest, 1)
+            OB[f * sub:(f + 1) * sub, main:] = tail[:, :rest].astype(BF16)
 
         S2[...] = (matmul(OB[...], ao[...]) + stream[...].reshape(crowd, chans).astype(F32)).astype(BF16)
         normalise(lambda s: S2[s, :].astype(F32))
@@ -442,11 +476,12 @@
             V((STEPS, width, chans), F32),
             V((STEPS, 16, chans), F32),
             V((chans, chans), BF16),
-            V((chans, 128), BF16),
-            V((128, chans), BF16),
+            V((nsh * chans, 128), BF16),
+            V((128, nsh * chans), BF16),
             V((crowd, chans), BF16),
             V((crowd, chans), F32), V((crowd, chans), F32), V((crowd, chans), F32),
-            V((nsh * crowd, chans), BF16), V((nsh * crowd, chans), BF16),
+            V((sub, nsh * rest), F32), V((sub, nsh * rest), F32),
+            V((2 * crowd, nsh * chans), BF16), V((crowd, 128), BF16),
             V((crowd, chans), BF16), V((crowd, chans), BF16), V((crowd, inner), BF16),
             V((3, 3 * chans, chans), BF16), V((3, 3 * chans, chans), BF16),
             V((3 * chans, -(-3 * rest // 128) * 128), BF16), V((3 * chans, -(-3 * rest // 128) * 128), BF16),

time: 69.9 us -> 69.6 us (level)
  no operation moved by 1% of the time
where the time goes in v3:
time: 69.6 us; the launch traced here: 69.5 us
  Pallas kernels  67.7 us (97%)
  local copies, waits for them, and re-layouts  1.78 us (3%)
    pallas_call x1, Pallas kernels, per_device(): pl.pallas_call(functools.partial(kernel, dims), out_shape=jax.ShapeDtypeS...  67.7 us
    unnamed x1, local copies, waits for them, and re-layouts  1.78 us

profile of v3, /device:TPU:0, one launch (start us, length us, event | category | flops | bytes accessed | tf_op | source)
XLA Modules:
  0.0 69.5 jit_solution(11445102194737541062)
XLA Ops:
  0.0 67.7 %shard_map.91 = bf16[512,320]{1,0:T(8,128)(2,1)} custom-call(s32[1,2]{1,0:T(1,128)} %stamps.1, bf16[512,320]{1,0:T(8,128)(2,1)} %bitcast.17, bf16[3,3,320,320]{3,2,1,0:T(8,128)(2,1)} %bitcast.11, bf16[3,3,320,320]{3,2,1,0:T(8,128)(2,1)} %bitcast.12, bf16[320,320]{1,0:T(8,128)(2,1)} %bitcast.18, bf16[320,960]{1,0:T(8,128)(2,1)} %bitcast.16, ...), custom_call_target="tpu_custom_call" | custom-call | tf_op jit(solution)/shard_map/pallas_call | solution.py:494
  67.7 1.8 %copy.11 = bf16[1,1,8,64,320]{4,3,2,1,0:T(8,128)(2,1)} copy(bf16[1,1,8,64,320]{4,3,2,1,0:T(8,128)(2,1)} %bitcast.14) | data formatting | bytes 655360
